TPU v7x, 512 devices: a whole 4x4x16 slice. The times are simulated.
512 devices in a mesh: row: 16 (over y, x_lo, core), col: 32 (over z, x_hi).
Axes of the slice: x: 4 (x_hi: 2, x_lo: 2; x = x_hi * 2 + x_lo), y: 4, z: 16, core: 2. Of those that a mesh axis runs over, the one named last changes fastest.
Arguments:
- traces: float32 [1024, 4096], P(('row', 'col')), may hold values from -6 to 6
- offsets: int32 [1024, 8], P(('row', 'col')), may hold values from 0 to 3072, as said below
- band_lo: int32 [1024], P(('row', 'col')), may hold values from 0 to 63
- band_hi: int32 [1024], P(('row', 'col')), may hold values from 192 to 256
- live: int32 [1024], P(('row', 'col')), may hold values 0 or 1
Outputs:
- correlations: bfloat16 [1024, 32, 16, 2, 512], P('row', 'col')
Inputs may be any that keep to these rules, and one draw needn't show every extreme that they name: `offsets`: every offset is a multiple of 256.
All inputs are finite; a program needn't handle non-finite values. No bound on the sum of `live` on one device may be relied on, other than what follows from the above.
Results may differ from a plain program's by a relative error of at most 0.0052.
Values may be sent and summed in bfloat16 or wider, within the bound.
A program may use at most 64 MiB of HBM per device.

v0:
```python
import math

import jax
import jax.numpy as jnp
from jax import lax
from jax.sharding import PartitionSpec as P

SEG = 8
SAMPLES = 1024
BINS = 256
LAGS = 512
TRACE = 4096


def sent_to_all(x, axis):
    devices = lax.axis_size(axis)
    return lax.all_to_all(jnp.broadcast_to(x[None], (devices, *x.shape)), axis, 0, 0, tiled=True)


def laid_out(pieces, dim):
    dims = list(pieces.shape[1:])
    dims[dim] *= pieces.shape[0]
    return jnp.moveaxis(pieces, 0, dim).reshape(dims)


def gather_directly(x, axis, dim):
    pieces = sent_to_all(x, axis)
    return laid_out(pieces, dim)


def transform_table():
    times = jnp.arange(SAMPLES, dtype=jnp.int32)
    freqs = jnp.arange(BINS, dtype=jnp.int32) + 1
    phase = jnp.mod(times[:, None] * freqs[None, :], SAMPLES).astype(jnp.float32) * (
        2.0 * math.pi / SAMPLES
    )
    taper = 0.5 - 0.5 * jnp.cos(times.astype(jnp.float32) * (2.0 * math.pi / SAMPLES))
    return jnp.concatenate([jnp.cos(phase), -jnp.sin(phase)], axis=1) * taper[:, None]


def lag_table():
    freqs = jnp.arange(BINS, dtype=jnp.int32) + 1
    shifts = jnp.arange(LAGS, dtype=jnp.int32) - LAGS // 2
    phase = jnp.mod(freqs[:, None] * shifts[None, :], SAMPLES).astype(jnp.float32) * (
        2.0 * math.pi / SAMPLES
    )
    return jnp.concatenate([jnp.cos(phase), -jnp.sin(phase)], axis=0) * (
        1.0 / math.sqrt(SEG * BINS)
    )


def cut_segments(traces, offsets):
    count = traces.shape[0]
    quarter = SAMPLES // 4
    block_count = TRACE // quarter
    blocks = traces.reshape(count, 1, block_count, quarter)
    first_block = offsets // quarter
    segment = jnp.zeros((count, SEG, 4, quarter), jnp.float32)
    for place in range(block_count - 3):
        picked = (first_block == place)[:, :, None, None]
        segment = jnp.where(picked, blocks[:, :, place : place + 4, :], segment)
    return segment.reshape(count * SEG, SAMPLES)


def whiten(traces, offsets, band_lo, band_hi, live):
    count = traces.shape[0]
    flat = cut_segments(traces, offsets)
    spec = jnp.dot(flat, transform_table(), precision=lax.Precision.HIGHEST)
    spec_re = spec[:, :BINS]
    spec_im = spec[:, BINS:]
    amp = jnp.sqrt(spec_re * spec_re + spec_im * spec_im)
    padded = jnp.pad(amp, ((0, 0), (2, 2)))
    smooth = (
        padded[:, 0:BINS]
        + padded[:, 1 : BINS + 1]
        + padded[:, 2 : BINS + 2]
        + padded[:, 3 : BINS + 3]
        + padded[:, 4 : BINS + 4]
    ) / 5.0
    level = jnp.mean(amp, axis=1, keepdims=True)
    factor = 1.0 / (smooth + 0.1 * level + 1e-06)
    bins = jnp.arange(BINS, dtype=jnp.int32)
    inside = (
        (bins[None, :] >= band_lo[:, None])
        & (bins[None, :] < band_hi[:, None])
        & (live[:, None] == 1)
    )
    keep = inside.astype(jnp.float32)
    factor = factor.reshape(count, SEG, BINS) * keep[:, None, :]
    spec = spec.reshape(count, SEG, 2 * BINS)
    white = spec * jnp.concatenate([factor, factor], axis=2)
    return white.astype(jnp.bfloat16)


def correlate(first, second, table):
    first_re, first_im = (first[..., :BINS], first[..., BINS:])
    second_re, second_im = (second[..., :BINS], second[..., BINS:])
    count_i, count_j = (first.shape[0], second.shape[0])
    cross_re = jnp.zeros((count_i, count_j, BINS), jnp.float32)
    cross_im = jnp.zeros((count_i, count_j, BINS), jnp.float32)
    for seg_index in range(SEG):
        left_re = first_re[:, None, seg_index, :].astype(jnp.float32)
        left_im = first_im[:, None, seg_index, :].astype(jnp.float32)
        right_re = second_re[None, :, seg_index, :].astype(jnp.float32)
        right_im = second_im[None, :, seg_index, :].astype(jnp.float32)
        cross_re = cross_re + (left_re * right_re + left_im * right_im)
        cross_im = cross_im + (left_im * right_re - left_re * right_im)
    cross = jnp.concatenate([cross_re, cross_im], axis=2)
    corr = jnp.dot(
        cross.reshape(count_i * count_j, 2 * BINS), table, precision=lax.Precision.HIGHEST
    )
    return corr.astype(jnp.bfloat16).reshape(count_i, count_j, LAGS)


def body(traces, offsets, band_lo, band_hi, live):
    white = whiten(traces, offsets, band_lo, band_hi, live)
    table = lag_table()
    first_panel = gather_directly(white, "col", 0)
    stacked = correlate(first_panel, lax.all_gather(white, "row", axis=0, tiled=True), table)
    channel_count = white.shape[0]
    return stacked.reshape(stacked.shape[0], 1, lax.axis_size("row"), channel_count, LAGS)


def solution(mesh):
    in_specs = (
        P(("row", "col"), None),
        P(("row", "col"), None),
        P(("row", "col")),
        P(("row", "col")),
        P(("row", "col")),
    )
    out_specs = P("row", "col", None, None, None)
    return jax.shard_map(body, mesh=mesh, in_specs=in_specs, out_specs=out_specs, check_vma=False)
```

profile of v0, /device:TPU:24, one launch (start us, length us, event | category | flops | bytes accessed | tf_op | source)
XLA Modules:
  0.0 75.8 jit_solution(12472655420938415955)
XLA Ops:
  0.0 0.7 broadcast_compare_fusion.13
  0.7 0.7 broadcast_compare_fusion.9
  1.4 0.1 broadcast_in_dim.248
  1.5 0.1 broadcast_in_dim.253
  1.6 0.1 broadcast_in_dim.303
  1.7 0.1 broadcast_in_dim.298
  1.8 0.1 broadcast_in_dim.293
  1.8 0.1 broadcast_in_dim.288
  1.9 0.1 broadcast_in_dim.283
  2.0 0.1 broadcast_in_dim.278
  2.1 0.1 broadcast_in_dim.273
  2.2 0.1 broadcast_in_dim.268
  2.3 0.1 broadcast_in_dim.263
  2.4 0.1 broadcast_in_dim.258
  2.4 0.1 broadcast_in_dim.308
  2.5 0.8 %copy.74 = f32[1,2,16,256]{3,2,1,0:T(8,128)S(1)} copy(f32[1,2,16,256]{3,1,2,0:T(2,128)} %bitcast.134) | data formatting | bytes 65536
  3.3 4.1 %fusion.23 = (f32[1024,256]{1,0:T(8,128)S(1)}, f32[1024,256]{1,0:T(8,128)S(1)}) fusion(s32[256]{0:T(256)S(1)} %iota_add_fusion.1), kind=kLoop, calls=%fused_computation.35 | loop fusion | flops 3932160 | bytes 2098176 | tf_op jit(solution)/shard_map/cos | solution.py:38
  7.6 1.3 %fusion.7 = f32[16,512]{1,0:T(8,128)S(1)} fusion(f32[1024,256]{1,0:T(8,128)S(1)} %get-tuple-element.69, f32[1024,256]{1,0:T(8,128)S(1)} %get-tuple-element.68, f32[1024]{0:T(1024)S(1)} %multiply_subtract_fusion, f32[16,1024]{1,0:T(8,128)S(1)} %bitcast.133, f32[16,1024]{1,0:T(8,128)S(1)} %bitcast.132, f32[16,1024]{1,0:T(8,128)S(1)} %bitcast.131, ...), kind=kOutput, calls=%fused_computation.6 | convolution fusion | flops 101924864 | bytes 2986192 | tf_op jit(solution)/shard_map/dot_general | solution.py:68
  9.0 0.1 fusion.67
  9.1 0.1 and_convert_fusion
  9.2 0.1 bitcast_multiply_fusion
  9.3 0.9 %broadcast_in_dim.314 = bf16[32,2,8,512]{3,2,1,0:T(8,128)(2,1)} broadcast(bf16[2,8,512]{2,1,0:T(8,128)(2,1)S(1)} %fusion.38), dimensions={1,2,3} | broadcast | bytes 540672 | tf_op jit(solution)/shard_map/broadcast_in_dim | solution.py:17
  10.2 17.9 %all-to-all-start = ((bf16[32,2,8,512]{3,2,1,0:T(8,128)(2,1)}), bf16[32,2,8,512]{3,2,1,0:T(8,128)(2,1)S(1)}, u32[]{:S(2)}, u32[]{:S(2)}) async-start(bf16[32,2,8,512]{3,2,1,0:T(8,128)(2,1)} %broadcast_in_dim.314), calls=%async_computation | async-start | bytes 1048576 | tf_op jit(solution)/shard_map/all_to_all | solution.py:17
  28.1 17.6 %all_gather.3 = bf16[32,8,512]{2,1,0:T(8,128)(2,1)S(1)} all-gather(bf16[2,8,512]{2,1,0:T(8,128)(2,1)S(1)} %fusion.38), channel_id=1, replica_groups=mesh['row'=16,'col'=32] {'row'}, dimensions={0}, use_global_device_ids=true | all-gather | bytes 278528 | tf_op jit(solution)/shard_map/all_gather | solution.py:119
  45.7 0.5 slice_convert_fusion.31
  46.3 2.1 %fusion.24 = (f32[256,512]{1,0:T(8,128)S(1)}, f32[256,512]{1,0:T(8,128)S(1)}) fusion(s32[512]{0:T(512)S(1)} %iota_add_fusion, s32[256]{0:T(256)S(1)} %iota_add_fusion.1), kind=kLoop, calls=%fused_computation.36 | loop fusion | flops 1966080 | bytes 1051648 | tf_op jit(solution)/shard_map/cos | solution.py:47
  48.4 12.7 %all-to-all-done = bf16[32,2,8,512]{3,2,1,0:T(8,128)(2,1)S(1)} async-done(((bf16[32,2,8,512]{3,2,1,0:T(8,128)(2,1)}), bf16[32,2,8,512]{3,2,1,0:T(8,128)(2,1)S(1)}, u32[]{:S(2)}, u32[]{:S(2)}) %all-to-all-start) | async-done | bytes 524320 | tf_op jit(solution)/shard_map/all_to_all | solution.py:17
  61.1 1.0 %slice_convert_fusion.15 = (f32[64,1,256]{2,1,0:T(1,128)S(1)}, f32[64,1,256]{2,1,0:T(1,128)S(1)}, f32[64,1,256]{2,1,0:T(1,128)S(1)}, f32[64,1,256]{2,1,0:T(1,128...) fusion(bf16[64,8,512]{2,1,0:T(8,128)(2,1)S(1)} %bitcast.117), kind=kLoop, calls=%fused_computation.52 | loop fusion | flops 262144 | bytes 1572864 | tf_op jit(solution)/shard_map/mul | solution.py:106
  62.2 2.2 %add_add_fusion = f32[64,32,256]{2,1,0:T(8,128)S(1)} fusion(f32[32,256]{1,0:T(8,128)S(1)} %get-tuple-element.70, f32[64,256]{1,0:T(8,128)S(1)} %get-tuple-element.86, f32[32,256]{1,0:T(8,128)S(1)} %get-tuple-element.71, f32[64,256]{1,0:T(8,128)S(1)} %get-tuple-element.87, f32[32,256]{1,0:T(8,128)S(1)} %get-tuple-element.72, ...), kind=kLoop, calls=%fused_computation.9 | loop fusion | flops 16252928 | bytes 3670016 | tf_op jit(solution)/shard_map/add | solution.py:107
  64.4 2.2 %add_add_fusion.1 = f32[64,32,256]{2,1,0:T(8,128)S(1)} fusion(f32[32,256]{1,0:T(8,128)S(1)} %get-tuple-element.70, f32[64,256]{1,0:T(8,128)S(1)} %get-tuple-element.86, f32[32,256]{1,0:T(8,128)S(1)} %get-tuple-element.71, f32[64,256]{1,0:T(8,128)S(1)} %get-tuple-element.87, f32[32,256]{1,0:T(8,128)S(1)} %get-tuple-element.72, ...), kind=kLoop, calls=%fused_computation.10 | loop fusion | flops 16252928 | bytes 3670016 | tf_op jit(solution)/shard_map/add | solution.py:106
  66.7 7.0 %fusion.4 = bf16[2048,512]{1,0:T(8,128)(2,1)S(1)} fusion(f32[2048,256]{1,0:T(8,128)S(1)} %bitcast.118, f32[2048,256]{1,0:T(8,128)S(1)} %bitcast.119, f32[256,512]{1,0:T(8,128)S(1)} %get-tuple-element.55, f32[256,512]{1,0:T(8,128)S(1)} %get-tuple-element.54), kind=kOutput, calls=%fused_computation.4 | convolution fusion | flops 6445072384 | bytes 7340032 | tf_op jit(solution)/shard_map/dot_general | solution.py:109
  73.6 2.2 %reshape_reshape.3 = bf16[64,1,16,2,512]{4,3,2,0,1:T(2,128)(2,1)} reshape(bf16[2048,512]{1,0:T(8,128)(2,1)S(1)} %fusion.4) | data formatting | bytes 4194304 | tf_op jit(solution)/shard_map/reshape;reshape | solution.py:121
  (40 shorter events, 0.3 us)
Async XLA Ops:
  7.4 1.7 %copy-start = (s32[2]{0:T(128)S(1)}, s32[2]{0:T(128)}, u32[]{:S(2)}) copy-start(s32[2]{0:T(128)} %param.8) | copy-start | bytes 28
  7.4 1.7 %copy-start.1 = (s32[2]{0:T(128)S(1)}, s32[2]{0:T(128)}, u32[]{:S(2)}) copy-start(s32[2]{0:T(128)} %param.7) | copy-start | bytes 28
  10.2 51.0 %all-to-all-start = ((bf16[32,2,8,512]{3,2,1,0:T(8,128)(2,1)}), bf16[32,2,8,512]{3,2,1,0:T(8,128)(2,1)S(1)}, u32[]{:S(2)}, u32[]{:S(2)}) async-start(bf16[32,2,8,512]{3,2,1,0:T(8,128)(2,1)} %broadcast_in_dim.314), calls=%async_computation | async-start | bytes 1048576 | tf_op jit(solution)/shard_map/all_to_all | solution.py:17
where the time goes:
time: 76.1 us; the launch traced here: 75.8 us
  starting transfers between devices  17.9 us (24%)
  blocking collectives  17.6 us (23%)
  other arithmetic  13.8 us (18%)
  waiting for transfers between devices  12.7 us (17%)
  matrix products  8.27 us (11%)
  local copies, waits for them, and re-layouts  5.18 us (7%)
    all_to_all x1, starting transfers between devices, sent_to_all(): lax.all_to_all(jnp.broadcast_to(x[None], (devices, *x.shape)), axis, 0, 0...  17.9 us
    all_gather x1, blocking collectives, body(): lax.all_gather(white, 'row', axis=0, tiled=True)  17.6 us
    all_to_all x1, waiting for transfers between devices, sent_to_all(): lax.all_to_all(jnp.broadcast_to(x[None], (devices, *x.shape)), axis, 0, 0...  12.7 us
    dot_general x1, matrix products, correlate(): jnp.dot(cross.reshape(count_i * count_j, 2 * BINS), table, precision=lax....  6.96 us
    cos x1, other arithmetic, transform_table(): jnp.cos(phase)  4.13 us
    another operation x1, local copies, waits for them, and re-layouts, body(): stacked.reshape(stacked.shape[0], 1, lax.axis_size('row'), channel_count,...  2.21 us
    add x1, other arithmetic, correlate(): cross_im = cross_im + (left_im * right_re - left_re * right_im)  2.21 us
    add x1, other arithmetic, correlate(): cross_re = cross_re + (left_re * right_re + left_im * right_im)  2.21 us
  transfers between devices with their start and end apart: 1, of which 1 were waited for; matrix products, arithmetic and copies ran while one was open for 4% of the time, Pallas kernels for 0%

commit v1 on v0

v1 whole, which is shorter than its diff:
```python
import functools
import math

import jax
import jax.numpy as jnp
import numpy as np
from jax import lax
from jax.experimental import pallas as pl
from jax.experimental.pallas import tpu as pltpu
from jax.sharding import PartitionSpec as P

SEG = 8
SAMPLES = 1024
QUARTER = SAMPLES // 4
BINS = 256
LAGS = 512
TRACE = 4096
CH_DEV = 2
ROWS = CH_DEV * SEG
MESH = pl.DeviceIdType.MESH

NZ, NY = 16, 4
N_ROW, N_COL = 16, 32
PANEL = N_COL * CH_DEV
SECOND = N_ROW * CH_DEV

GROUPS = (
    ((0, 0), (0, 1), (1, 0), (-1, 0)),
    ((1, 1), (-1, 1), (3, 0), (-3, 0)),
    ((6, 0), (-6, 0), (8, 0), (8, 1)),
    ((3, 1), (2, 0), (4, 0), (-3, 1)),
    ((-2, 0), (-4, 0), (2, 1), (4, 1)),
    ((-2, 1), (-4, 1), (6, 1), (-6, 1)),
    ((5, 0), (7, 0), (-5, 0), (-7, 0)),
    ((5, 1), (7, 1), (-5, 1), (-7, 1)),
)
SLOT = {d: n for n, d in enumerate(d for group in GROUPS for d in group)}
FAR = ((8, 1), (8, 0), (6, 0), (-6, 0), (3, 0), (-3, 0))
NEAR = ((1, 0), (-1, 0), (0, 1), (1, 1), (-1, 1))
RELAYED = ((3, 0), (-3, 0), (6, 0), (-6, 0))
COL_STEPS = tuple(dict.fromkeys(FAR + NEAR))
ROW_STEPS = tuple(
    (dy, dx, dc) for dy in (2, 1, -1, 0) for dx in (1, 0) for dc in (0, 1) if (dy, dx, dc) != (0, 0, 0)
)


def dft_table():
    times = np.arange(QUARTER)
    freqs = np.arange(BINS) + 1
    phase = (times[:, None] * freqs[None, :] % SAMPLES) * (2.0 * math.pi / SAMPLES)
    return np.concatenate([np.cos(phase), -np.sin(phase)], axis=1).astype(np.float32)


def taper_table():
    times = np.arange(SAMPLES)
    return (0.5 - 0.5 * np.cos(times * (2.0 * math.pi / SAMPLES))).reshape(4, QUARTER).astype(np.float32)


def lag_table():
    freqs = np.arange(BINS) + 1
    shifts = np.arange(LAGS) - LAGS // 2
    phase = np.mod(freqs[:, None] * shifts[None, :], SAMPLES) * (2.0 * math.pi / SAMPLES)
    return np.concatenate([np.cos(phase), -np.sin(phase)], axis=0).astype(np.float32)


def col_device(step, sign=1):
    col = lax.axis_index("col")
    z = lax.rem(col // 2 + sign * step[0] + 2 * NZ, NZ)
    x = lax.rem(col % 2 + step[1], 2)
    return {"col": z * 2 + x}


def row_device(step, sign=1):
    row = lax.axis_index("row")
    y = lax.rem(row // 4 + sign * step[0] + NY, NY)
    x = lax.rem((row // 2) % 2 + step[1], 2)
    core = lax.rem(row % 2 + step[2], 2)
    return {"row": (y * 2 + x) * 2 + core}


def whiten(traces, offsets, band_lo, band_hi, live, taper, dft, pieces):
    sub = lax.broadcasted_iota(jnp.int32, (SEG, BINS), 0)
    for k in range(CH_DEV):
        start = jnp.zeros((SEG, BINS), jnp.int32)
        for s in range(SEG):
            start = jnp.where(sub == s, offsets[k, s], start)
        cut = [jnp.zeros((SEG, QUARTER), jnp.float32) for _ in range(4)]
        for block in range(TRACE // QUARTER):
            samples = jnp.broadcast_to(
                traces[k : k + 1, block * QUARTER : (block + 1) * QUARTER], (SEG, QUARTER)
            )
            for q in range(4):
                place = block - q
                if 0 <= place <= TRACE // QUARTER - 4:
                    cut[q] = jnp.where(start == place * QUARTER, samples, cut[q])
        for q in range(4):
            row = q * ROWS + k * SEG
            pieces[row : row + SEG, :] = cut[q] * taper[q : q + 1, :]
    parts = jnp.dot(
        pieces[...], dft[...], precision=lax.Precision.HIGHEST, preferred_element_type=jnp.float32
    )
    lane = lax.broadcasted_iota(jnp.int32, (ROWS, BINS), 1)
    spec_re = parts[:ROWS, :BINS]
    spec_im = parts[:ROWS, BINS:]
    for q in range(1, 4):
        part_re = parts[q * ROWS : (q + 1) * ROWS, :BINS]
        part_im = parts[q * ROWS : (q + 1) * ROWS, BINS:]
        turn = ((lane + 1) * q) & 3
        spec_re = spec_re + jnp.where(
            turn == 0, part_re, jnp.where(turn == 1, part_im, jnp.where(turn == 2, -part_re, -part_im))
        )
        spec_im = spec_im + jnp.where(
            turn == 0, part_im, jnp.where(turn == 1, -part_re, jnp.where(turn == 2, -part_im, part_re))
        )
    amp = jnp.sqrt(spec_re * spec_re + spec_im * spec_im)

    def moved(by):
        return jnp.where((lane >= by) & (lane < BINS + by), pltpu.roll(amp, by % BINS, 1), 0.0)

    smooth = (moved(2) + moved(1) + amp + moved(-1) + moved(-2)) / 5.0
    level = jnp.sum(amp, axis=1, keepdims=True) * (1.0 / BINS)
    factor = 1.0 / (smooth + 0.1 * level + 1e-06)
    first = lax.broadcasted_iota(jnp.int32, (ROWS, BINS), 0) < SEG
    low = jnp.where(first, band_lo[0], band_lo[1])
    high = jnp.where(first, band_hi[0], band_hi[1])
    alive = jnp.where(first, live[0], live[1])
    inside = (lane >= low) & (lane < high) & (alive == 1)
    factor = factor * jnp.where(inside, 1.0, 0.0)
    return jnp.concatenate([spec_re * factor, spec_im * factor], axis=1).astype(jnp.bfloat16)


def kernel(
    offsets_in, band_lo_in, band_hi_in, live_in, traces_in, taper_in, dft_in, lags_in, out,
    offsets, band_lo, band_hi, live, traces, taper, dft, lags, load_sem, pieces, firsts, seconds, first_f32, second_f32, second_mix, cross,
    first_send, first_recv, second_send, second_recv,
):
    loads = [
        pltpu.make_async_copy(source, target, load_sem.at[n])
        for n, (source, target) in enumerate(
            (
                (traces_in, traces), (offsets_in, offsets), (band_lo_in, band_lo), (band_hi_in, band_hi),
                (live_in, live), (taper_in, taper), (dft_in, dft), (lags_in, lags),
            )
        )
    ]
    for load in loads:
        load.start()
    barrier = pltpu.get_barrier_semaphore()
    for step in COL_STEPS:
        pl.semaphore_signal(barrier, inc=1, device_id=col_device(step, -1), device_id_type=MESH)
    for step in ROW_STEPS:
        pl.semaphore_signal(barrier, inc=1, device_id=row_device(step, -1), device_id_type=MESH)

    for load in loads[:-1]:
        load.wait()
    white = whiten(traces, offsets, band_lo, band_hi, live, taper, dft, pieces)
    my_row = lax.axis_index("row")
    firsts[0] = white
    seconds[my_row] = white
    pl.semaphore_wait(barrier, len(COL_STEPS) + len(ROW_STEPS))

    def first_copy(held, step):
        slot = SLOT[(held[0] + step[0], (held[1] + step[1]) % 2)]
        return pltpu.make_async_remote_copy(
            src_ref=firsts.at[SLOT[held]],
            dst_ref=firsts.at[slot],
            send_sem=first_send.at[slot],
            recv_sem=first_recv.at[slot],
            device_id=col_device(step),
            device_id_type=MESH,
        )

    copies = {}
    for step in FAR + NEAR:
        copies[step] = first_copy((0, 0), step)
    second_copies = []
    for n, step in enumerate(ROW_STEPS):
        second_copies.append(
            pltpu.make_async_remote_copy(
                src_ref=firsts.at[0],
                dst_ref=seconds.at[my_row],
                send_sem=second_send.at[n],
                recv_sem=second_recv.at[n],
                device_id=row_device(step),
                device_id_type=MESH,
            )
        )
    for step in FAR:
        copies[step].start()
    for copy in second_copies:
        copy.start()
    for step in NEAR:
        copies[step].start()

    arrived = {(0, 0)}

    def take(place):
        if place not in arrived:
            arrived.add(place)
            copies[place].wait_recv()

    for place in RELAYED:
        take(place)
        for step in NEAR:
            copy = first_copy(place, step)
            copies[(place[0] + step[0], (place[1] + step[1]) % 2)] = copy
            copy.start()

    for copy in second_copies:
        copy.wait_recv()

    @pl.loop(0, N_ROW)
    def _(n):
        block = seconds[n].astype(jnp.float32) * (1.0 / math.sqrt(SEG * BINS))
        for tile in range(4):
            at = pl.ds(pl.multiple_of(n * ROWS, ROWS), ROWS)
            second_f32[tile, at, :] = block[:, tile * 128 : tile * 128 + 128]

    @pl.loop(0, SEG)
    def _(s):
        for tile in range(2):
            re = second_f32[tile, pl.ds(s, SECOND, stride=SEG), :]
            im = second_f32[2 + tile, pl.ds(s, SECOND, stride=SEG), :]
            second_mix[0, s, :, tile * 128 : tile * 128 + 128] = re
            second_mix[1, s, :, tile * 128 : tile * 128 + 128] = re - im
            second_mix[2, s, :, tile * 128 : tile * 128 + 128] = re + im

    loads[-1].wait()
    my_col = lax.axis_index("col")
    for g, group in enumerate(GROUPS):
        for place in group:
            take(place)

        @pl.loop(0, len(group))
        def _(t):
            block = firsts[g * 4 + t].astype(jnp.float32)
            for tile in range(4):
                first_f32[tile] = block[:, tile * 128 : tile * 128 + 128]
            for tile in range(2):
                first_f32[4 + tile] = (
                    block[:, tile * 128 : tile * 128 + 128] + block[:, BINS + tile * 128 : BINS + tile * 128 + 128]
                )
            for half in range(2):
                lo = half * 128
                total = [[[None] * 4 for _ in range(3)] for _ in range(CH_DEV)]
                for s in range(SEG):
                    b = [
                        [second_mix[m, s, jt * 8 : jt * 8 + 8, lo : lo + 128] for jt in range(4)]
                        for m in range(3)
                    ]
                    for k in range(CH_DEV):
                        row = k * SEG + s
                        a = [
                            first_f32[4 + half, pl.ds(row, 8, stride=0), :],
                            first_f32[2 + half, pl.ds(row, 8, stride=0), :],
                            first_f32[half, pl.ds(row, 8, stride=0), :],
                        ]
                        for m in range(3):
                            for jt in range(4):
                                term = a[m] * b[m][jt]
                                old = total[k][m][jt]
                                total[k][m][jt] = term if old is None else old + term
                for k in range(CH_DEV):
                    for pair in range(2):
                        re = [total[k][0][jt] - total[k][1][jt] for jt in (2 * pair, 2 * pair + 1)]
                        im = [total[k][0][jt] - total[k][2][jt] for jt in (2 * pair, 2 * pair + 1)]
                        at = pl.multiple_of(t * 64 + k * 32 + pair * 16, 16)
                        cross[pl.ds(at, 16), lo : lo + 128] = jnp.concatenate(re, 0).astype(jnp.bfloat16)
                        cross[pl.ds(at, 16), BINS + lo : BINS + lo + 128] = jnp.concatenate(im, 0).astype(
                            jnp.bfloat16
                        )

        corr = jnp.dot(cross[...], lags[...], preferred_element_type=jnp.float32).astype(jnp.bfloat16)
        for t, (dz, dx) in enumerate(group):
            source = lax.rem(my_col // 2 - dz + 2 * NZ, NZ) * 2 + lax.rem(my_col % 2 + dx, 2)
            out[pl.ds(source * 2, 2), 0] = corr[t * 64 : t * 64 + 64].reshape(2, N_ROW, CH_DEV, LAGS)

    for copy in copies.values():
        copy.wait_send()
    for copy in second_copies:
        copy.wait_send()


def body(traces, offsets, band_lo, band_hi, live):
    vmem = pl.BlockSpec(memory_space=pltpu.VMEM)
    hbm = pl.BlockSpec(memory_space=pltpu.HBM)
    stacked = pl.pallas_call(
        kernel,
        out_shape=jax.ShapeDtypeStruct((PANEL, 1, N_ROW, CH_DEV, LAGS), jnp.bfloat16),
        in_specs=[hbm] * 8,
        out_specs=vmem,
        scratch_shapes=[
            pltpu.SMEM((CH_DEV, SEG), jnp.int32),
            pltpu.SMEM((CH_DEV,), jnp.int32),
            pltpu.SMEM((CH_DEV,), jnp.int32),
            pltpu.SMEM((CH_DEV,), jnp.int32),
            pltpu.VMEM((CH_DEV, TRACE), jnp.float32),
            pltpu.VMEM((4, QUARTER), jnp.float32),
            pltpu.VMEM((QUARTER, 2 * BINS), jnp.float32),
            pltpu.VMEM((2 * BINS, LAGS), jnp.bfloat16),
            pltpu.SemaphoreType.DMA((8,)),
            pltpu.VMEM((4 * ROWS, QUARTER), jnp.float32),
            pltpu.VMEM((N_COL, ROWS, 2 * BINS), jnp.bfloat16),
            pltpu.VMEM((N_ROW, ROWS, 2 * BINS), jnp.bfloat16),
            pltpu.VMEM((6, ROWS, 128), jnp.float32),
            pltpu.VMEM((4, N_ROW * ROWS, 128), jnp.float32),
            pltpu.VMEM((3, SEG, SECOND, BINS), jnp.float32),
            pltpu.VMEM((256, 2 * BINS), jnp.bfloat16),
            pltpu.SemaphoreType.DMA((N_COL,)),
            pltpu.SemaphoreType.DMA((N_COL,)),
            pltpu.SemaphoreType.DMA((N_ROW,)),
            pltpu.SemaphoreType.DMA((N_ROW,)),
        ],
        compiler_params=pltpu.CompilerParams(collective_id=0, has_side_effects=True, vmem_limit_bytes=16 << 20),
        name="stack",
    )(
        *(
            pltpu.with_memory_space_constraint(operand, pltpu.HBM)
            for operand in (
                offsets, band_lo, band_hi, live, traces,
                jnp.asarray(taper_table()), jnp.asarray(dft_table()), jnp.asarray(lag_table(), jnp.bfloat16),
            )
        )
    )
    return stacked


def solution(mesh):
    in_specs = (
        P(("row", "col"), None),
        P(("row", "col"), None),
        P(("row", "col")),
        P(("row", "col")),
        P(("row", "col")),
    )
    out_specs = P("row", "col", None, None, None)
    return jax.shard_map(body, mesh=mesh, in_specs=in_specs, out_specs=out_specs, check_vma=False)
```

time: 76.1 us -> 34.9 us (0.46)
  Pallas kernels: 0 us -> 32.9 us
  starting transfers between devices: 17.9 us -> 0 us
  blocking collectives: 17.6 us -> 0 us
  other arithmetic: 13.8 us -> 0 us
  waiting for transfers between devices: 12.7 us -> 0 us
  matrix products: 8.27 us -> 0 us
  local copies, waits for them, and re-layouts: 5.18 us -> 1.32 us
    pallas_call x0 -> x1, Pallas kernels: none -> 32.9 us  [body(): pl.pallas_call(kernel, out_shape=jax.ShapeDtypeStruct((PANEL, 1, N_ROW, C...]
    all_to_all x1 -> x0, starting transfers between devices: 17.9 us -> none  [sent_to_all(): lax.all_to_all(jnp.broadcast_to(x[None], (devices, *x.shape)), axis, 0, 0...]
    all_gather x1 -> x0, blocking collectives: 17.6 us -> none  [body(): lax.all_gather(white, 'row', axis=0, tiled=True)]
    all_to_all x1 -> x0, waiting for transfers between devices: 12.7 us -> none  [sent_to_all(): lax.all_to_all(jnp.broadcast_to(x[None], (devices, *x.shape)), axis, 0, 0...]
    dot_general x2 -> x0, matrix products: 8.27 us -> none  [the longest x1 6.96 us: correlate(): jnp.dot(cross.reshape(count_i * count_j, 2 * BINS), table, precision=lax....]
    cos x2 -> x0, other arithmetic: 6.26 us -> none  [the longest x1 4.13 us: transform_table(): jnp.cos(phase)]
    add x3 -> x0, other arithmetic: 4.42 us -> none  [the longest x1 2.21 us: correlate(): cross_im = cross_im + (left_im * right_re - left_re * right_im)]
    another operation x1 -> x0, local copies, waits for them, and re-layouts: 2.21 us -> none  [body(): stacked.reshape(stacked.shape[0], 1, lax.axis_size('row'), channel_count,...]
  transfers between devices with their start and end apart: 1 -> 0, of which waited for: 1 -> 0; matrix products, arithmetic and copies ran while one was open for 4% -> 0% of each run, Pallas kernels for 0% -> 0%
where the time goes in v1:
time: 34.9 us; the launch traced here: 34.2 us
  Pallas kernels  32.9 us (94%)
  local copies, waits for them, and re-layouts  1.32 us (4%)
    pallas_call x1, Pallas kernels, body(): pl.pallas_call(kernel, out_shape=jax.ShapeDtypeStruct((PANEL, 1, N_ROW, C...  32.9 us
    unnamed x1, local copies, waits for them, and re-layouts  1.32 us

profile of v1, /device:TPU:24, one launch (start us, length us, event | category | flops | bytes accessed | tf_op | source)
XLA Modules:
  0.0 34.2 jit_solution(6510518728198014893)
XLA Ops:
  0.0 32.9 %stack.1 = bf16[64,1,16,2,512]{4,3,2,1,0:T(2,128)(2,1)S(1)} custom-call(s32[2,8]{1,0:T(2,128)} %offsets_in.1, s32[2]{0:T(128)} %band_lo_in.1, s32[2]{0:T(128)} %band_hi_in.1, s32[2]{0:T(128)} %live_in.1, f32[2,4096]{1,0:T(2,128)} %traces_in.1, f32[4,256]{1,0:T(4,128)} %constant.6.clone.taper_in, f32[256,512]{1,0:T(8,128)} %constant.7.clone.dft_in, ...), custom_call_target="tpu_custom_call" | custom-call | tf_op jit(solution)/shard_map/stack/pallas_call | solution.py:287
  32.9 1.3 %copy.10 = bf16[64,1,16,2,512]{4,3,2,1,0:T(2,128)(2,1)} copy(bf16[64,1,16,2,512]{4,3,2,1,0:T(2,128)(2,1)S(1)} %stack.1) | data formatting | bytes 4194304

commit v2 on v1

--- a/solution.py
+++ b/solution.py
@@ -23,22 +23,24 @@
 N_ROW, N_COL = 16, 32
 PANEL = N_COL * CH_DEV
 SECOND = N_ROW * CH_DEV
+PAIRS = CH_DEV * SECOND
 
 GROUPS = (
-    ((0, 0), (0, 1), (1, 0), (-1, 0)),
-    ((1, 1), (-1, 1), (3, 0), (-3, 0)),
-    ((6, 0), (-6, 0), (8, 0), (8, 1)),
-    ((3, 1), (2, 0), (4, 0), (-3, 1)),
-    ((-2, 0), (-4, 0), (2, 1), (4, 1)),
-    ((-2, 1), (-4, 1), (6, 1), (-6, 1)),
-    ((5, 0), (7, 0), (-5, 0), (-7, 0)),
-    ((5, 1), (7, 1), (-5, 1), (-7, 1)),
+    ((0, 0), (1, 0), (-1, 0), (0, 1)),
+    ((2, 0), (-2, 0), (1, 1), (-1, 1)),
+    ((2, 1), (-2, 1), (5, 0), (-5, 0)),
+    ((4, 0), (6, 0), (-4, 0), (-6, 0)),
+    ((5, 1), (-5, 1), (3, 0), (-3, 0)),
+    ((7, 0), (-7, 0), (4, 1), (6, 1)),
+    ((-4, 1), (-6, 1), (8, 0), (3, 1)),
+    ((-3, 1), (7, 1), (-7, 1), (8, 1)),
 )
-SLOT = {d: n for n, d in enumerate(d for group in GROUPS for d in group)}
-FAR = ((8, 1), (8, 0), (6, 0), (-6, 0), (3, 0), (-3, 0))
-NEAR = ((1, 0), (-1, 0), (0, 1), (1, 1), (-1, 1))
-RELAYED = ((3, 0), (-3, 0), (6, 0), (-6, 0))
-COL_STEPS = tuple(dict.fromkeys(FAR + NEAR))
+PLACES = tuple(d for group in GROUPS for d in group)
+SLOT = {d: n for n, d in enumerate(PLACES)}
+FAR = ((5, 0), (-5, 0))
+NEAR = ((2, 1), (-2, 1), (1, 1), (-1, 1), (2, 0), (-2, 0), (0, 1), (1, 0), (-1, 0))
+RELAYS = {(5, 0): ((3, 1), (3, 0)) + NEAR, (-5, 0): NEAR}
+COL_STEPS = FAR + NEAR + ((3, 0), (3, 1))
 ROW_STEPS = tuple(
     (dy, dx, dc) for dy in (2, 1, -1, 0) for dx in (1, 0) for dc in (0, 1) if (dy, dx, dc) != (0, 0, 0)
 )
@@ -78,7 +80,7 @@
     return {"row": (y * 2 + x) * 2 + core}
 
 
-def whiten(traces, offsets, band_lo, band_hi, live, taper, dft, pieces):
+def whiten(traces, offsets, band_lo, band_hi, live, taper, dft, pieces, dft_load):
     sub = lax.broadcasted_iota(jnp.int32, (SEG, BINS), 0)
     for k in range(CH_DEV):
         start = jnp.zeros((SEG, BINS), jnp.int32)
@@ -96,6 +98,7 @@
         for q in range(4):
             row = q * ROWS + k * SEG
             pieces[row : row + SEG, :] = cut[q] * taper[q : q + 1, :]
+    dft_load.wait()
     parts = jnp.dot(
         pieces[...], dft[...], precision=lax.Precision.HIGHEST, preferred_element_type=jnp.float32
     )
@@ -131,7 +134,7 @@
 
 def kernel(
     offsets_in, band_lo_in, band_hi_in, live_in, traces_in, taper_in, dft_in, lags_in, out,
-    offsets, band_lo, band_hi, live, traces, taper, dft, lags, load_sem, pieces, firsts, seconds, first_f32, second_f32, second_mix, cross,
+    offsets, band_lo, band_hi, live, traces, taper, dft, lags, load_sem, pieces, firsts, seconds, first_f32, second_mix, cross_a, cross_b,
     first_send, first_recv, second_send, second_recv,
 ):
     loads = [
@@ -151,9 +154,9 @@
     for step in ROW_STEPS:
         pl.semaphore_signal(barrier, inc=1, device_id=row_device(step, -1), device_id_type=MESH)
 
-    for load in loads[:-1]:
+    for load in loads[:-2]:
         load.wait()
-    white = whiten(traces, offsets, band_lo, band_hi, live, taper, dft, pieces)
+    white = whiten(traces, offsets, band_lo, band_hi, live, taper, dft, pieces, loads[-2])
     my_row = lax.axis_index("row")
     firsts[0] = white
     seconds[my_row] = white
@@ -199,9 +202,9 @@
             arrived.add(place)
             copies[place].wait_recv()
 
-    for place in RELAYED:
+    for place, steps in RELAYS.items():
         take(place)
-        for step in NEAR:
+        for step in steps:
             copy = first_copy(place, step)
             copies[(place[0] + step[0], (place[1] + step[1]) % 2)] = copy
             copy.start()
@@ -212,68 +215,84 @@
     @pl.loop(0, N_ROW)
     def _(n):
         block = seconds[n].astype(jnp.float32) * (1.0 / math.sqrt(SEG * BINS))
-        for tile in range(4):
-            at = pl.ds(pl.multiple_of(n * ROWS, ROWS), ROWS)
-            second_f32[tile, at, :] = block[:, tile * 128 : tile * 128 + 128]
-
-    @pl.loop(0, SEG)
-    def _(s):
-        for tile in range(2):
-            re = second_f32[tile, pl.ds(s, SECOND, stride=SEG), :]
-            im = second_f32[2 + tile, pl.ds(s, SECOND, stride=SEG), :]
-            second_mix[0, s, :, tile * 128 : tile * 128 + 128] = re
-            second_mix[1, s, :, tile * 128 : tile * 128 + 128] = re - im
-            second_mix[2, s, :, tile * 128 : tile * 128 + 128] = re + im
+        for k in range(CH_DEV):
+            for tile in range(2):
+                re = block[k * SEG : k * SEG + SEG, tile * 128 : tile * 128 + 128]
+                im = block[k * SEG : k * SEG + SEG, BINS + tile * 128 : BINS + tile * 128 + 128]
+                at = pl.ds(n * 2 + k, SEG, stride=SECOND)
+                for m, mixed in enumerate((re, re - im, re + im)):
+                    second_mix[2 * m + tile, at, :] = mixed
 
     loads[-1].wait()
     my_col = lax.axis_index("col")
+
+    def source_of(place):
+        return lax.rem(my_col // 2 - place[0] + 2 * NZ, NZ) * 2 + lax.rem(my_col % 2 + place[1], 2)
+
+    crosses = (cross_a, cross_b)
+
+    def cross_block(n, v, buffer, base):
+        block = firsts[n].astype(jnp.float32)
+        for tile in range(4):
+            first_f32[6 * v + tile] = block[:, tile * 128 : tile * 128 + 128]
+        for tile in range(2):
+            lo = tile * 128
+            first_f32[6 * v + 4 + tile] = block[:, lo : lo + 128] + block[:, BINS + lo : BINS + lo + 128]
+        for half in range(2):
+            lo = half * 128
+            total = [[[None] * 4 for _ in range(3)] for _ in range(CH_DEV)]
+            for s in range(SEG):
+                b = [
+                    [second_mix[2 * m + half, s * SECOND + jt * 8 : s * SECOND + jt * 8 + 8, :] for jt in range(4)]
+                    for m in range(3)
+                ]
+                for k in range(CH_DEV):
+                    row = k * SEG + s
+                    a = [first_f32[6 * v + tile + half, pl.ds(row, 8, stride=0), :] for tile in (4, 2, 0)]
+                    for m in range(3):
+                        for jt in range(4):
+                            term = a[m] * b[m][jt]
+                            old = total[k][m][jt]
+                            total[k][m][jt] = term if old is None else old + term
+            for k in range(CH_DEV):
+                for pair in range(2):
+                    tiles = (2 * pair, 2 * pair + 1)
+                    re = [total[k][0][jt] - total[k][1][jt] for jt in tiles]
+                    im = [total[k][0][jt] - total[k][2][jt] for jt in tiles]
+                    at = pl.ds(pl.multiple_of(base + k * SECOND + pair * 16, 16), 16)
+                    buffer[at, lo : lo + 128] = jnp.concatenate(re, 0).astype(jnp.bfloat16)
+                    buffer[at, BINS + lo : BINS + lo + 128] = jnp.concatenate(im, 0).astype(jnp.bfloat16)
+
+    def lag_half(g, u):
+        at = pl.ds(pl.multiple_of(u * 256, 256), 256)
+        corr = jnp.dot(crosses[g % 2][...], lags[:, at], preferred_element_type=jnp.float32)
+        corr = corr.astype(jnp.bfloat16)
+        for t, place in enumerate(GROUPS[g]):
+            rows = corr[t * PAIRS : (t + 1) * PAIRS].reshape(CH_DEV, N_ROW, CH_DEV, 256)
+            out[pl.ds(source_of(place) * 2, 2), 0, :, :, at] = rows
+
+    def step(g, u):
+        if g > 0:
+            lag_half(g - 1, u)
+        for v in range(2):
+            t = 2 * u + v
+            cross_block(g * 4 + t, v, crosses[g % 2], t * PAIRS)
+
     for g, group in enumerate(GROUPS):
-        for place in group:
-            take(place)
-
-        @pl.loop(0, len(group))
-        def _(t):
-            block = firsts[g * 4 + t].astype(jnp.float32)
-            for tile in range(4):
-                first_f32[tile] = block[:, tile * 128 : tile * 128 + 128]
-            for tile in range(2):
-                first_f32[4 + tile] = (
-                    block[:, tile * 128 : tile * 128 + 128] + block[:, BINS + tile * 128 : BINS + tile * 128 + 128]
-                )
-            for half in range(2):
-                lo = half * 128
-                total = [[[None] * 4 for _ in range(3)] for _ in range(CH_DEV)]
-                for s in range(SEG):
-                    b = [
-                        [second_mix[m, s, jt * 8 : jt * 8 + 8, lo : lo + 128] for jt in range(4)]
-                        for m in range(3)
-                    ]
-                    for k in range(CH_DEV):
-                        row = k * SEG + s
-                        a = [
-                            first_f32[4 + half, pl.ds(row, 8, stride=0), :],
-                            first_f32[2 + half, pl.ds(row, 8, stride=0), :],
-                            first_f32[half, pl.ds(row, 8, stride=0), :],
-                        ]
-                        for m in range(3):
-                            for jt in range(4):
-                                term = a[m] * b[m][jt]
-                                old = total[k][m][jt]
-                                total[k][m][jt] = term if old is None else old + term
-                for k in range(CH_DEV):
-                    for pair in range(2):
-                        re = [total[k][0][jt] - total[k][1][jt] for jt in (2 * pair, 2 * pair + 1)]
-                        im = [total[k][0][jt] - total[k][2][jt] for jt in (2 * pair, 2 * pair + 1)]
-                        at = pl.multiple_of(t * 64 + k * 32 + pair * 16, 16)
-                        cross[pl.ds(at, 16), lo : lo + 128] = jnp.concatenate(re, 0).astype(jnp.bfloat16)
-                        cross[pl.ds(at, 16), BINS + lo : BINS + lo + 128] = jnp.concatenate(im, 0).astype(
-                            jnp.bfloat16
-                        )
-
-        corr = jnp.dot(cross[...], lags[...], preferred_element_type=jnp.float32).astype(jnp.bfloat16)
-        for t, (dz, dx) in enumerate(group):
-            source = lax.rem(my_col // 2 - dz + 2 * NZ, NZ) * 2 + lax.rem(my_col % 2 + dx, 2)
-            out[pl.ds(source * 2, 2), 0] = corr[t * 64 : t * 64 + 64].reshape(2, N_ROW, CH_DEV, LAGS)
+        if g < len(GROUPS) - 2:
+            for place in group:
+                take(place)
+
+            @pl.loop(0, 2)
+            def _(u):
+                step(g, u)
+        else:
+            for u in range(2):
+                take(group[2 * u])
+                take(group[2 * u + 1])
+                step(g, u)
+    for u in range(2):
+        lag_half(len(GROUPS) - 1, u)
 
     for copy in copies.values():
         copy.wait_send()
@@ -302,10 +321,10 @@
             pltpu.VMEM((4 * ROWS, QUARTER), jnp.float32),
             pltpu.VMEM((N_COL, ROWS, 2 * BINS), jnp.bfloat16),
             pltpu.VMEM((N_ROW, ROWS, 2 * BINS), jnp.bfloat16),
-            pltpu.VMEM((6, ROWS, 128), jnp.float32),
-            pltpu.VMEM((4, N_ROW * ROWS, 128), jnp.float32),
-            pltpu.VMEM((3, SEG, SECOND, BINS), jnp.float32),
-            pltpu.VMEM((256, 2 * BINS), jnp.bfloat16),
+            pltpu.VMEM((12, ROWS, 128), jnp.float32),
+            pltpu.VMEM((6, SEG * SECOND, 128), jnp.float32),
+            pltpu.VMEM((4 * PAIRS, 2 * BINS), jnp.bfloat16),
+            pltpu.VMEM((4 * PAIRS, 2 * BINS), jnp.bfloat16),
             pltpu.SemaphoreType.DMA((N_COL,)),
             pltpu.SemaphoreType.DMA((N_COL,)),
             pltpu.SemaphoreType.DMA((N_ROW,)),

time: 34.9 us -> 32.5 us (0.931)
  Pallas kernels: 32.9 us -> 30.6 us
    pallas_call x1, Pallas kernels: 32.9 us -> 30.6 us  [body(): pl.pallas_call(kernel, out_shape=jax.ShapeDtypeStruct((PANEL, 1, N_ROW, C...]
where the time goes in v2:
time: 32.5 us; the launch traced here: 32 us
  Pallas kernels  30.6 us (94%)
  local copies, waits for them, and re-layouts  1.32 us (4%)
    pallas_call x1, Pallas kernels, body(): pl.pallas_call(kernel, out_shape=jax.ShapeDtypeStruct((PANEL, 1, N_ROW, C...  30.6 us
    unnamed x1, local copies, waits for them, and re-layouts  1.32 us

profile of v2, /device:TPU:24, one launch (start us, length us, event | category | flops | bytes accessed | tf_op | source)
XLA Modules:
  0.0 32.0 jit_solution(13329822517847041074)
XLA Ops:
  0.0 30.6 %stack.1 = bf16[64,1,16,2,512]{4,3,2,1,0:T(2,128)(2,1)S(1)} custom-call(s32[2,8]{1,0:T(2,128)} %offsets_in.1, s32[2]{0:T(128)} %band_lo_in.1, s32[2]{0:T(128)} %band_hi_in.1, s32[2]{0:T(128)} %live_in.1, f32[2,4096]{1,0:T(2,128)} %traces_in.1, f32[4,256]{1,0:T(4,128)} %constant.6.clone.taper_in, f32[256,512]{1,0:T(8,128)} %constant.7.clone.dft_in, ...), custom_call_target="tpu_custom_call" | custom-call | tf_op jit(solution)/shard_map/stack/pallas_call | solution.py:306
  30.6 1.3 %copy.10 = bf16[64,1,16,2,512]{4,3,2,1,0:T(2,128)(2,1)} copy(bf16[64,1,16,2,512]{4,3,2,1,0:T(2,128)(2,1)S(1)} %stack.1) | data formatting | bytes 4194304

commit v3 on v2

--- a/solution.py
+++ b/solution.py
@@ -38,8 +38,8 @@
 PLACES = tuple(d for group in GROUPS for d in group)
 SLOT = {d: n for n, d in enumerate(PLACES)}
 FAR = ((5, 0), (-5, 0))
-NEAR = ((2, 1), (-2, 1), (1, 1), (-1, 1), (2, 0), (-2, 0), (0, 1), (1, 0), (-1, 0))
-RELAYS = {(5, 0): ((3, 1), (3, 0)) + NEAR, (-5, 0): NEAR}
+NEAR = ((1, 0), (-1, 0), (2, 0), (-2, 0), (0, 1), (1, 1), (-1, 1), (2, 1), (-2, 1))
+RELAYS = {(5, 0): NEAR[:4] + ((3, 0),) + NEAR[4:] + ((3, 1),), (-5, 0): NEAR}
 COL_STEPS = FAR + NEAR + ((3, 0), (3, 1))
 ROW_STEPS = tuple(
     (dy, dx, dc) for dy in (2, 1, -1, 0) for dx in (1, 0) for dc in (0, 1) if (dy, dx, dc) != (0, 0, 0)
@@ -209,19 +209,20 @@
             copies[(place[0] + step[0], (place[1] + step[1]) % 2)] = copy
             copy.start()
 
-    for copy in second_copies:
-        copy.wait_recv()
-
-    @pl.loop(0, N_ROW)
-    def _(n):
-        block = seconds[n].astype(jnp.float32) * (1.0 / math.sqrt(SEG * BINS))
+    def mix(row):
+        block = seconds[row].astype(jnp.float32) * (1.0 / math.sqrt(SEG * BINS))
         for k in range(CH_DEV):
             for tile in range(2):
                 re = block[k * SEG : k * SEG + SEG, tile * 128 : tile * 128 + 128]
                 im = block[k * SEG : k * SEG + SEG, BINS + tile * 128 : BINS + tile * 128 + 128]
-                at = pl.ds(n * 2 + k, SEG, stride=SECOND)
+                at = pl.ds(row * 2 + k, SEG, stride=SECOND)
                 for m, mixed in enumerate((re, re - im, re + im)):
                     second_mix[2 * m + tile, at, :] = mixed
+
+    mix(my_row)
+    for n in range(len(ROW_STEPS) - 1, -1, -1):
+        second_copies[n].wait_recv()
+        mix(row_device(ROW_STEPS[n], -1)["row"])
 
     loads[-1].wait()
     my_col = lax.axis_index("col")

time: 32.5 us -> 31.8 us (0.978)
  Pallas kernels: 30.6 us -> 30.2 us
    pallas_call x1, Pallas kernels: 30.6 us -> 30.2 us  [body(): pl.pallas_call(kernel, out_shape=jax.ShapeDtypeStruct((PANEL, 1, N_ROW, C...]
where the time goes in v3:
time: 31.8 us; the launch traced here: 31.5 us
  Pallas kernels  30.2 us (95%)
  local copies, waits for them, and re-layouts  1.32 us (4%)
    pallas_call x1, Pallas kernels, body(): pl.pallas_call(kernel, out_shape=jax.ShapeDtypeStruct((PANEL, 1, N_ROW, C...  30.2 us
    unnamed x1, local copies, waits for them, and re-layouts  1.32 us

profile of v3, /device:TPU:24, one launch (start us, length us, event | category | flops | bytes accessed | tf_op | source)
XLA Modules:
  0.0 31.5 jit_solution(4431244433671617194)
XLA Ops:
  0.0 30.2 %stack.1 = bf16[64,1,16,2,512]{4,3,2,1,0:T(2,128)(2,1)S(1)} custom-call(s32[2,8]{1,0:T(2,128)} %offsets_in.1, s32[2]{0:T(128)} %band_lo_in.1, s32[2]{0:T(128)} %band_hi_in.1, s32[2]{0:T(128)} %live_in.1, f32[2,4096]{1,0:T(2,128)} %traces_in.1, f32[4,256]{1,0:T(4,128)} %constant.6.clone.taper_in, f32[256,512]{1,0:T(8,128)} %constant.7.clone.dft_in, ...), custom_call_target="tpu_custom_call" | custom-call | tf_op jit(solution)/shard_map/stack/pallas_call | solution.py:307
  30.2 1.3 %copy.10 = bf16[64,1,16,2,512]{4,3,2,1,0:T(2,128)(2,1)} copy(bf16[64,1,16,2,512]{4,3,2,1,0:T(2,128)(2,1)S(1)} %stack.1) | data formatting | bytes 4194304

commit v4 on v3

--- a/solution.py
+++ b/solution.py
@@ -30,8 +30,8 @@
     ((2, 0), (-2, 0), (1, 1), (-1, 1)),
     ((2, 1), (-2, 1), (5, 0), (-5, 0)),
     ((4, 0), (6, 0), (-4, 0), (-6, 0)),
-    ((5, 1), (-5, 1), (3, 0), (-3, 0)),
-    ((7, 0), (-7, 0), (4, 1), (6, 1)),
+    ((3, 0), (-3, 0), (7, 0), (-7, 0)),
+    ((5, 1), (-5, 1), (4, 1), (6, 1)),
     ((-4, 1), (-6, 1), (8, 0), (3, 1)),
     ((-3, 1), (7, 1), (-7, 1), (8, 1)),
 )

time: 31.8 us -> 31.8 us (level)
  no operation moved by 1% of the time
where the time goes in v4:
time: 31.8 us; the launch traced here: 31.5 us
  Pallas kernels  30.2 us (95%)
  local copies, waits for them, and re-layouts  1.32 us (4%)
    pallas_call x1, Pallas kernels, body(): pl.pallas_call(kernel, out_shape=jax.ShapeDtypeStruct((PANEL, 1, N_ROW, C...  30.2 us
    unnamed x1, local copies, waits for them, and re-layouts  1.32 us

profile of v4, /device:TPU:24, one launch (start us, length us, event | category | flops | bytes accessed | tf_op | source)
XLA Modules:
  0.0 31.5 jit_solution(5912533353845882818)
XLA Ops:
  0.0 30.2 %stack.1 = bf16[64,1,16,2,512]{4,3,2,1,0:T(2,128)(2,1)S(1)} custom-call(s32[2,8]{1,0:T(2,128)} %offsets_in.1, s32[2]{0:T(128)} %band_lo_in.1, s32[2]{0:T(128)} %band_hi_in.1, s32[2]{0:T(128)} %live_in.1, f32[2,4096]{1,0:T(2,128)} %traces_in.1, f32[4,256]{1,0:T(4,128)} %constant.6.clone.taper_in, f32[256,512]{1,0:T(8,128)} %constant.7.clone.dft_in, ...), custom_call_target="tpu_custom_call" | custom-call | tf_op jit(solution)/shard_map/stack/pallas_call | solution.py:307
  30.2 1.3 %copy.10 = bf16[64,1,16,2,512]{4,3,2,1,0:T(2,128)(2,1)} copy(bf16[64,1,16,2,512]{4,3,2,1,0:T(2,128)(2,1)S(1)} %stack.1) | data formatting | bytes 4194304
